TPU v7x, 32 devices: a whole 2x2x4 slice. The times are simulated.
32 devices in a mesh: groups: 2 (over y), seq: 16 (over z, x, core).
Axes of the slice: x: 2, y: 2, z: 4, core: 2. Of those that a mesh axis runs over, the one named last changes fastest.
Arguments:
- residual: bfloat16 [8192, 1024], P(('groups', 'seq')), parts along dimension 0, may hold values from -6 to 6
- layer_queries: bfloat16 [8192, 512], P(('groups', 'seq')), parts along dimension 0, may hold values from -200 to 200
- layer_keyvals: bfloat16 [8192, 256], P(('groups', 'seq')), parts along dimension 0, may hold values from -8 to 8
- head_window_extent: int32 [8], replicated, may hold values from 32 to 256, as said below
- block_mask: int32 [16, 4], P('seq'), may hold values 0 or 1
- first_out: bfloat16 [512, 1024], replicated, may hold values from -1 to 1
- second_query: bfloat16 [1024, 512], replicated, may hold values from -12 to 12
- second_keyval: bfloat16 [1024, 256], replicated, may hold values from -1 to 1
- second_out: bfloat16 [512, 1024], replicated, may hold values from -1 to 1
Outputs:
- layer_output: bfloat16 [8192, 1024], P(('groups', 'seq')), parts along dimension 0
There are 2 independent parts, one for each index of `groups`. A program takes and returns all parts, laid end to end along the dimension named above; an argument that names none is the same for every part. Nothing has to cross between parts.
Inputs may be any that keep to these rules, and one draw needn't show every extreme that they name: `head_window_extent`: per head; some head has exactly 256 and some exactly 32.
All inputs are finite; a program needn't handle non-finite values. No bound on the sum of `block_mask` on one device may be relied on, other than what follows from the above.
Results may differ from a plain program's by a relative error of at most 0.0065.
Values may be sent and summed in bfloat16 or wider, within the bound.
A program may use at most 64 MiB of HBM per device.

v0:
```python
import functools

import jax
import jax.numpy as jnp
from jax import lax
from jax.experimental import pallas as pl
from jax.experimental.pallas import tpu as pltpu
from jax.sharding import PartitionSpec as P

QUERY_HEADS = 8
HEAD_SIZE = 64
MESH = pl.DeviceIdType.MESH
HIDE = -1e30
TOTALS = 16
NT = (((1,), (1,)), ((), ()))


def dot_nt(a, b):
    return lax.dot_general(a, b, NT, preferred_element_type=jnp.float32)


def dot(a, b):
    return jnp.dot(a, b, preferred_element_type=jnp.float32)


def rolled(x):
    return jnp.concatenate([x[:, HEAD_SIZE:], x[:, :HEAD_SIZE]], axis=1)


def spread(keys, values, ones, kx, vt, slot):
    low = lax.broadcasted_iota(jnp.int32, keys.shape, 1) < HEAD_SIZE
    none = jnp.zeros_like(keys)
    first, second = jnp.where(low, keys, none), jnp.where(low, none, keys)
    kx[slot, 0, 0] = first
    kx[slot, 0, 1] = rolled(first)
    kx[slot, 1, 0] = rolled(second)
    kx[slot, 1, 1] = second
    for group in range(2):
        vt[slot, group, :HEAD_SIZE] = values[group * HEAD_SIZE : (group + 1) * HEAD_SIZE]
        vt[slot, group, HEAD_SIZE:] = ones


def col_max(parts):
    top = jnp.max(parts[0], axis=0, keepdims=True)
    for part in parts[1:]:
        top = jnp.maximum(top, jnp.max(part, axis=0, keepdims=True))
    return top


def weight(scores, top):
    return jnp.exp((scores - top).astype(jnp.bfloat16))


def staggered(steps, scores, weigh, finish):
    ready, weighed = {}, {}
    count = len(steps)
    for at in range(count + 2):
        if at < count:
            ready[at] = scores(steps[at])
        if 0 <= at - 1 < count:
            weighed[at - 1] = weigh(steps[at - 1], ready.pop(at - 1))
        if 0 <= at - 2 < count:
            finish(steps[at - 2], *weighed.pop(at - 2))


def shared(acc):
    return acc[:HEAD_SIZE] * (1.0 / acc[HEAD_SIZE : HEAD_SIZE + 1])


def body(
    n, levels,
    q_hbm, kv_hbm, res_hbm, extent, mask, wo1_hbm, wq2_hbm, wkv2_hbm,
    att_out, hid_out,
    q, kv, halo, res, wo1, wq2, wkv2, kv2, kv2_in, kx, vt, tops, accs, att, hid,
    local_sem, send_sem, recv_sem,
):
    rows = q.shape[0]
    wide = 2 * HEAD_SIZE
    pairs = q.shape[1] // wide
    per_group = pairs // 2
    scaled = jnp.bfloat16(HEAD_SIZE ** (-0.5))
    me = lax.axis_index("seq")
    loads = [
        pltpu.make_async_copy(src, dst, local_sem.at[i])
        for i, (src, dst) in enumerate(
            (
                (kv_hbm, kv),
                (q_hbm, q),
                (wo1_hbm, wo1),
                (res_hbm, res),
                (wkv2_hbm, wkv2),
                (wq2_hbm, wq2),
            )
        )
    ]
    barrier = pltpu.get_barrier_semaphore()
    has_left, has_right = me > 0, me < n - 1

    @pl.when(has_left)
    def _():
        pl.semaphore_signal(barrier, inc=1, device_id={"seq": me - 1}, device_id_type=MESH)

    @pl.when(has_right)
    def _():
        pl.semaphore_signal(barrier, inc=1, device_id={"seq": me + 1}, device_id_type=MESH)

    def partner(level):
        bit = lax.rem(lax.div(me, 1 << level), 2)
        return me + (1 << level) * (1 - 2 * bit)

    for level in range(levels):
        pl.semaphore_signal(barrier, inc=1, device_id={"seq": partner(level)}, device_id_type=MESH)
    for load in loads:
        load.start()
    ends = has_left.astype(jnp.int32) + has_right.astype(jnp.int32)
    pl.semaphore_wait(barrier, levels + ends)

    def to_right():
        return pltpu.make_async_remote_copy(
            kv_hbm, halo.at[0], send_sem.at[0], recv_sem.at[0],
            device_id={"seq": me + 1}, device_id_type=MESH,
        )

    def to_left():
        return pltpu.make_async_remote_copy(
            kv_hbm, halo.at[1], send_sem.at[1], recv_sem.at[1],
            device_id={"seq": me - 1}, device_id_type=MESH,
        )

    @pl.when(has_right)
    def _():
        to_right().start()

    @pl.when(has_left)
    def _():
        to_left().start()

    ones = jnp.ones((TOTALS, rows), jnp.bfloat16)

    loads[0].wait()
    spread(kv[:, :wide] * scaled, kv[:, wide:].T, ones, kx, vt, 0)
    loads[1].wait()
    key = lax.broadcasted_iota(jnp.int32, (rows, rows), 0)
    query = lax.broadcasted_iota(jnp.int32, (rows, rows), 1)
    apart = jnp.abs(key - query)
    heads = list(range(2 * pairs))

    def queries_of(h):
        pair = h // 2
        return q[:, pair * wide : (pair + 1) * wide]

    def put(h, share, halves, here):
        halves.append(share)
        if h % 2:
            both = jnp.concatenate(halves, axis=0).astype(jnp.bfloat16)
            att[here, h // 2 * wide : (h // 2 + 1) * wide] = both.T
            halves.clear()

    def own_scores(h):
        return dot_nt(kx[0, h // 2 // per_group, h % 2], queries_of(h))

    def own_weigh(h, scores):
        scores = jnp.where(apart <= extent[h], scores, HIDE)
        top = col_max([scores])
        tops[h] = jnp.broadcast_to(top, tops.shape[1:])
        return (weight(scores, top),)

    def own_finish(h, shares):
        accs[h] = dot(vt[0, h // 2 // per_group], shares)

    staggered(heads, own_scores, own_weigh, own_finish)

    @pl.when(has_left)
    def _():
        to_right().wait_recv()

    @pl.when(jnp.logical_not(has_left))
    def _():
        halo[0] = jnp.zeros(halo.shape[1:], jnp.bfloat16)

    @pl.when(has_right)
    def _():
        to_left().wait_recv()

    @pl.when(jnp.logical_not(has_right))
    def _():
        halo[1] = jnp.zeros(halo.shape[1:], jnp.bfloat16)

    for side in range(2):
        spread(halo[side, :, :wide] * scaled, halo[side, :, wide:].T, ones, kx, vt, 1 + side)
    far = 4 * n * rows
    left_off = rows + jnp.where(has_left, 0, far)
    right_off = rows + jnp.where(has_right, 0, far)
    tiles = rows // wide
    for i in (2, 3, 4):
        loads[i].wait()
    swaps = [
        [
            pltpu.make_async_remote_copy(
                kv2.at[pl.ds(tile * 2 * wide, 2 * wide)],
                kv2_in.at[level, pl.ds(tile * 2 * wide, 2 * wide)],
                send_sem.at[2 + level * tiles + tile],
                recv_sem.at[2 + level * tiles + tile],
                device_id={"seq": partner(level)}, device_id_type=MESH,
            )
            for tile in range(tiles)
        ]
        for level in range(levels)
    ]
    halves, normed, turned = [], [], []
    for tile in range(tiles):
        here = slice(tile * wide, (tile + 1) * wide)
        left = slice(tile * wide, rows)
        right = slice(0, (tile + 1) * wide)
        left_apart = (query - key)[left, here] + left_off
        right_apart = (key - query)[right, here] + right_off

        def side_scores(h):
            pair = h // 2
            queries = q[here, pair * wide : (pair + 1) * wide]
            return [
                dot_nt(kx[1, pair // per_group, h % 2, left], queries),
                dot_nt(kx[2, pair // per_group, h % 2, right], queries),
            ]

        def side_weigh(h, parts):
            a = jnp.where(left_apart <= extent[h], parts[0], HIDE)
            b = jnp.where(right_apart <= extent[h], parts[1], HIDE)
            before = tops[h, 0:1, here]
            top = jnp.maximum(before, col_max([a, b]))
            return jnp.exp(before - top), weight(a, top), weight(b, top)

        def side_finish(h, fade, a, b):
            acc = accs[h, :, here] * fade
            acc += dot(vt[1, h // 2 // per_group, :, left], a)
            acc += dot(vt[2, h // 2 // per_group, :, right], b)
            put(h, shared(acc), halves, here)

        staggered(heads, side_scores, side_weigh, side_finish)

        hidden = (dot(att[here], wo1[...]) + res[here].astype(jnp.float32)).astype(jnp.bfloat16)
        hid[here] = hidden
        values = hidden.astype(jnp.float32)
        scale = lax.rsqrt(jnp.mean(values * values, axis=-1, keepdims=True) + 1e-05)
        normed.append((values * scale).astype(jnp.bfloat16))
        keyvals = dot(normed[-1], wkv2[...]).astype(jnp.bfloat16)
        turned.append(keyvals[:, wide:].T)
        kv2[tile * 2 * wide : (tile * 2 + 1) * wide] = keyvals[:, :wide] * scaled
        kv2[(tile * 2 + 1) * wide : (tile * 2 + 2) * wide] = turned[-1]
        for swap in swaps:
            swap[tile].start()

    def keys_of(block):
        return jnp.concatenate([block[2 * t * wide : (2 * t + 1) * wide] for t in range(tiles)], axis=0)

    def values_of(block):
        return jnp.concatenate(
            [block[(2 * t + 1) * wide : (2 * t + 2) * wide] for t in range(tiles)], axis=1
        )

    keep_hidden = pltpu.make_async_copy(hid, hid_out, local_sem.at[6])
    keep_hidden.start()
    loads[5].wait()
    q[...] = dot(jnp.concatenate(normed, axis=0), wq2[...]).astype(jnp.bfloat16)
    spread(keys_of(kv2), values_of(kv2), ones, kx, vt, 0)

    chunks, first = [], 0
    while first <= levels:
        size = 2 if first + 1 < levels else 1
        chunks.append(list(range(first, first + size)))
        first += size
    for chunk in chunks:
        for slot in chunk:
            if slot > 0:
                for swap in swaps[slot - 1]:
                    swap.wait_recv()
                seen = mask[0, slot - 1] == 1
                came = values_of(kv2_in[slot - 1])
                spread(
                    jnp.where(seen, keys_of(kv2_in[slot - 1]), keys_of(kv2)),
                    jnp.where(seen, came, jnp.zeros_like(came)),
                    jnp.where(seen, ones, jnp.zeros_like(ones)),
                    kx, vt, slot,
                )

        def far_scores(h):
            return [dot_nt(kx[slot, h // 2 // per_group, h % 2], queries_of(h)) for slot in chunk]

        def far_weigh(h, parts):
            top = col_max(parts)
            fade = None
            if chunk[0] > 0:
                before = tops[h, 0:1]
                top = jnp.maximum(before, top)
                fade = jnp.exp(before - top)
            if chunk[-1] < levels:
                tops[h] = jnp.broadcast_to(top, tops.shape[1:])
            return fade, [weight(part, top) for part in parts]

        def far_finish(h, fade, parts):
            acc = None if fade is None else accs[h] * fade
            for slot, part in zip(chunk, parts):
                term = dot(vt[slot, h // 2 // per_group], part)
                acc = term if acc is None else acc + term
            if chunk[-1] < levels:
                accs[h] = acc
            else:
                put(h, shared(acc), halves, slice(0, rows))

        staggered(heads, far_scores, far_weigh, far_finish)

    keep_att = pltpu.make_async_copy(att, att_out, local_sem.at[7])
    keep_att.start()
    for level in swaps:
        for swap in level:
            swap.wait_send()

    @pl.when(has_right)
    def _():
        to_right().wait_send()

    @pl.when(has_left)
    def _():
        to_left().wait_send()

    keep_hidden.wait()
    keep_att.wait()


def shards(
    n, residual, layer_queries, layer_keyvals, head_window_extent, block_mask,
    first_out, second_query, second_keyval, second_out,
):
    levels = n.bit_length() - 1
    rows, width = residual.shape
    query_width = layer_queries.shape[1]
    kv_width = layer_keyvals.shape[1]
    wide = 2 * HEAD_SIZE
    blocks = max(3, levels + 1)
    bf16, f32 = jnp.bfloat16, jnp.float32
    anywhere = pl.BlockSpec(memory_space=pl.ANY)
    stays = pl.BlockSpec(memory_space=pltpu.HBM)
    scalars = pl.BlockSpec(memory_space=pltpu.SMEM)
    att, hidden = pl.pallas_call(
        functools.partial(body, n, levels),
        name="two_layers",
        out_shape=(
            jax.ShapeDtypeStruct((rows, query_width), bf16),
            jax.ShapeDtypeStruct((rows, width), bf16),
        ),
        in_specs=[stays] * 3 + [scalars] * 2 + [stays] * 3,
        out_specs=(anywhere, anywhere),
        scratch_shapes=[
            pltpu.VMEM((rows, query_width), bf16),
            pltpu.VMEM((rows, kv_width), bf16),
            pltpu.VMEM((2, rows, kv_width), bf16),
            pltpu.VMEM((rows, width), bf16),
            pltpu.VMEM(first_out.shape, bf16),
            pltpu.VMEM(second_query.shape, bf16),
            pltpu.VMEM(second_keyval.shape, bf16),
            pltpu.VMEM((2 * rows, wide), bf16),
            pltpu.VMEM((levels, 2 * rows, wide), bf16),
            pltpu.VMEM((blocks, 2, 2, rows, wide), bf16),
            pltpu.VMEM((blocks, 2, HEAD_SIZE + TOTALS, rows), bf16),
            pltpu.VMEM((QUERY_HEADS, 8, rows), f32),
            pltpu.VMEM((QUERY_HEADS, HEAD_SIZE + TOTALS, rows), f32),
            pltpu.VMEM((rows, query_width), bf16),
            pltpu.VMEM((rows, width), bf16),
            pltpu.SemaphoreType.DMA((8,)),
            pltpu.SemaphoreType.DMA((2 + levels * (rows // wide),)),
            pltpu.SemaphoreType.DMA((2 + levels * (rows // wide),)),
        ],
        compiler_params=pltpu.CompilerParams(
            collective_id=0, has_side_effects=True
        ),
    )(
        layer_queries, layer_keyvals, residual, head_window_extent, block_mask,
        first_out, second_query, second_keyval,
    )
    output = jnp.dot(att, second_out, preferred_element_type=f32) + hidden.astype(f32)
    return output.astype(bf16)


def solution(mesh):
    placed = (
        P(("groups", "seq"), None),
        P(("groups", "seq"), None),
        P(("groups", "seq"), None),
        P(),
        P("seq", None),
        P(),
        P(),
        P(),
        P(),
    )
    return jax.shard_map(
        functools.partial(shards, mesh.shape["seq"]),
        mesh=mesh, in_specs=placed, out_specs=P(("groups", "seq"), None), check_vma=False,
    )
```

profile of v0, /device:TPU:0, one launch (start us, length us, event | category | flops | bytes accessed | tf_op | source)
XLA Modules:
  0.0 23.9 jit_solution(4676791682282340828)
XLA Ops:
  0.0 0.0 copy-start
  0.0 21.5 %two_layers.1 = (bf16[256,512]{1,0:T(8,128)(2,1)}, bf16[256,1024]{1,0:T(8,128)(2,1)}) custom-call(bf16[256,512]{1,0:T(8,128)(2,1)} %q_hbm.1, bf16[256,256]{1,0:T(8,128)(2,1)} %kv_hbm.1, bf16[256,1024]{1,0:T(8,128)(2,1)} %res_hbm.1, s32[8]{0:T(128)} %extent.1, s32[1,4]{1,0:T(1,128)} %mask.1, bf16[512,1024]{1,0:T(8,128)(2,1)} %wo1_hbm.1, ...), custom_call_target="tpu_custom_call" | custom-call | tf_op jit(solution)/shard_map/two_layers/pallas_call | solution.py:344
  21.6 0.0 copy-done
  21.6 2.4 %fusion = bf16[256,1024]{1,0:T(8,128)(2,1)} fusion(bf16[256,512]{1,0:T(8,128)(2,1)} %get-tuple-element.7, bf16[512,1024]{1,0:T(8,128)(2,1)S(1)} %copy-done, bf16[256,1024]{1,0:T(8,128)(2,1)} %get-tuple-element.8), kind=kOutput, calls=%fused_computation.1 | convolution fusion | flops 269221888 | bytes 2359296 | tf_op jit(solution)/shard_map/dot_general | solution.py:380
Async XLA Ops:
  0.0 21.6 %copy-start = (bf16[512,1024]{1,0:T(8,128)(2,1)S(1)}, bf16[512,1024]{1,0:T(8,128)(2,1)}, u32[]{:S(2)}) copy-start(bf16[512,1024]{1,0:T(8,128)(2,1)} %param.17) | copy-start | bytes 3145732
where the time goes:
time: 24.1 us; the launch traced here: 23.9 us
  Pallas kernels  21.5 us (89%)
  matrix products  2.36 us (10%)
    pallas_call x1, Pallas kernels, shards(): pl.pallas_call(functools.partial(body, n, levels), name='two_layers', out...  21.5 us
    dot_general x1, matrix products, shards(): jnp.dot(att, second_out, preferred_element_type=f32) + hidden.astype(f32)  2.36 us

commit v1 on v0

--- a/solution.py
+++ b/solution.py
@@ -69,10 +69,10 @@
 
 def body(
     n, levels,
-    q_hbm, kv_hbm, res_hbm, extent, mask, wo1_hbm, wq2_hbm, wkv2_hbm,
-    att_out, hid_out,
-    q, kv, halo, res, wo1, wq2, wkv2, kv2, kv2_in, kx, vt, tops, accs, att, hid,
-    local_sem, send_sem, recv_sem,
+    q_hbm, kv_hbm, res_hbm, extent_hbm, mask_hbm, wo1_hbm, wq2_hbm, wkv2_hbm, wo2_hbm,
+    out_ref,
+    q, kv, halo, res, wo1, wq2, wkv2, wo2, kv2, kv2_in, kx, vt, tops, accs, att, hid,
+    extent, mask, local_sem, send_sem, recv_sem,
 ):
     rows = q.shape[0]
     wide = 2 * HEAD_SIZE
@@ -90,6 +90,9 @@
                 (res_hbm, res),
                 (wkv2_hbm, wkv2),
                 (wq2_hbm, wq2),
+                (wo2_hbm, wo2),
+                (extent_hbm, extent),
+                (mask_hbm, mask),
             )
         )
     ]
@@ -140,6 +143,8 @@
     loads[0].wait()
     spread(kv[:, :wide] * scaled, kv[:, wide:].T, ones, kx, vt, 0)
     loads[1].wait()
+    loads[8].wait()
+    loads[7].wait()
     key = lax.broadcasted_iota(jnp.int32, (rows, rows), 0)
     query = lax.broadcasted_iota(jnp.int32, (rows, rows), 1)
     apart = jnp.abs(key - query)
@@ -258,8 +263,6 @@
             [block[(2 * t + 1) * wide : (2 * t + 2) * wide] for t in range(tiles)], axis=1
         )
 
-    keep_hidden = pltpu.make_async_copy(hid, hid_out, local_sem.at[6])
-    keep_hidden.start()
     loads[5].wait()
     q[...] = dot(jnp.concatenate(normed, axis=0), wq2[...]).astype(jnp.bfloat16)
     spread(keys_of(kv2), values_of(kv2), ones, kx, vt, 0)
@@ -309,8 +312,9 @@
 
         staggered(heads, far_scores, far_weigh, far_finish)
 
-    keep_att = pltpu.make_async_copy(att, att_out, local_sem.at[7])
-    keep_att.start()
+    loads[6].wait()
+    final = (dot(att[...], wo2[...]) + hid[...].astype(jnp.float32)).astype(jnp.bfloat16)
+    out_ref[...] = final
     for level in swaps:
         for swap in level:
             swap.wait_send()
@@ -322,9 +326,6 @@
     @pl.when(has_left)
     def _():
         to_left().wait_send()
-
-    keep_hidden.wait()
-    keep_att.wait()
 
 
 def shards(
@@ -341,15 +342,12 @@
     anywhere = pl.BlockSpec(memory_space=pl.ANY)
     stays = pl.BlockSpec(memory_space=pltpu.HBM)
     scalars = pl.BlockSpec(memory_space=pltpu.SMEM)
-    att, hidden = pl.pallas_call(
+    return pl.pallas_call(
         functools.partial(body, n, levels),
         name="two_layers",
-        out_shape=(
-            jax.ShapeDtypeStruct((rows, query_width), bf16),
-            jax.ShapeDtypeStruct((rows, width), bf16),
-        ),
-        in_specs=[stays] * 3 + [scalars] * 2 + [stays] * 3,
-        out_specs=(anywhere, anywhere),
+        out_shape=pltpu.VMEM((rows, width), bf16),
+        in_specs=[stays] * 9,
+        out_specs=pl.BlockSpec(memory_space=pltpu.VMEM),
         scratch_shapes=[
             pltpu.VMEM((rows, query_width), bf16),
             pltpu.VMEM((rows, kv_width), bf16),
@@ -358,6 +356,7 @@
             pltpu.VMEM(first_out.shape, bf16),
             pltpu.VMEM(second_query.shape, bf16),
             pltpu.VMEM(second_keyval.shape, bf16),
+            pltpu.VMEM(second_out.shape, bf16),
             pltpu.VMEM((2 * rows, wide), bf16),
             pltpu.VMEM((levels, 2 * rows, wide), bf16),
             pltpu.VMEM((blocks, 2, 2, rows, wide), bf16),
@@ -366,7 +365,9 @@
             pltpu.VMEM((QUERY_HEADS, HEAD_SIZE + TOTALS, rows), f32),
             pltpu.VMEM((rows, query_width), bf16),
             pltpu.VMEM((rows, width), bf16),
-            pltpu.SemaphoreType.DMA((8,)),
+            pltpu.SMEM(head_window_extent.shape, jnp.int32),
+            pltpu.SMEM(block_mask.shape, jnp.int32),
+            pltpu.SemaphoreType.DMA((10,)),
             pltpu.SemaphoreType.DMA((2 + levels * (rows // wide),)),
             pltpu.SemaphoreType.DMA((2 + levels * (rows // wide),)),
         ],
@@ -375,10 +376,8 @@
         ),
     )(
         layer_queries, layer_keyvals, residual, head_window_extent, block_mask,
-        first_out, second_query, second_keyval,
+        first_out, second_query, second_keyval, second_out,
     )
-    output = jnp.dot(att, second_out, preferred_element_type=f32) + hidden.astype(f32)
-    return output.astype(bf16)
 
 
 def solution(mesh):

time: 24.1 us -> 21.3 us (0.88)
  matrix products: 2.36 us -> 0 us
  Pallas kernels: 21.5 us -> 20.4 us
  local copies, waits for them, and re-layouts: 0.01 us -> 0.8 us
    dot_general x1 -> x0, matrix products: 2.36 us -> none  [shards(): jnp.dot(att, second_out, preferred_element_type=f32) + hidden.astype(f32)]
    pallas_call x1, Pallas kernels: 21.5 us -> 20.4 us  [shards(): pl.pallas_call(functools.partial(body, n, levels), name='two_layers', out...]
    unnamed x2 -> x1, local copies, waits for them, and re-layouts: 0.01 us -> 0.8 us
where the time goes in v1:
time: 21.3 us; the launch traced here: 21.2 us
  Pallas kernels  20.4 us (96%)
  local copies, waits for them, and re-layouts  0.8 us (4%)
    pallas_call x1, Pallas kernels, shards(): pl.pallas_call(functools.partial(body, n, levels), name='two_layers', out...  20.4 us
    unnamed x1, local copies, waits for them, and re-layouts  0.8 us

profile of v1, /device:TPU:0, one launch (start us, length us, event | category | flops | bytes accessed | tf_op | source)
XLA Modules:
  0.0 21.2 jit_solution(3706381634104681892)
XLA Ops:
  0.0 20.4 %two_layers.1 = bf16[256,1024]{1,0:T(8,128)(2,1)S(1)} custom-call(bf16[256,512]{1,0:T(8,128)(2,1)} %q_hbm.1, bf16[256,256]{1,0:T(8,128)(2,1)} %kv_hbm.1, bf16[256,1024]{1,0:T(8,128)(2,1)} %res_hbm.1, s32[8]{0:T(128)} %extent_hbm.1, s32[1,4]{1,0:T(1,128)} %mask_hbm.1, bf16[512,1024]{1,0:T(8,128)(2,1)} %wo1_hbm.1, bf16[1024,512]{1,0:T(8,128)(2,1)} %wq2_hbm.1, ...), custom_call_target="tpu_custom_call" | custom-call | tf_op jit(solution)/shard_map/two_layers/pallas_call | solution.py:345
  20.4 0.8 %copy.11 = bf16[256,1024]{1,0:T(8,128)(2,1)} copy(bf16[256,1024]{1,0:T(8,128)(2,1)S(1)} %two_layers.1) | data formatting | bytes 1048576

commit v2 on v1

v2 whole, which is shorter than its diff:
```python
import functools

import jax
import jax.numpy as jnp
from jax import lax
from jax.experimental import pallas as pl
from jax.experimental.pallas import tpu as pltpu
from jax.sharding import PartitionSpec as P

QUERY_HEADS = 8
HEAD_SIZE = 64
WIDE = 2 * HEAD_SIZE
MESH = pl.DeviceIdType.MESH
HIDE = -1e30
TOTALS = 16
NT = (((1,), (1,)), ((), ()))


def dot_nt(a, b):
    return lax.dot_general(a, b, NT, preferred_element_type=jnp.float32)


def dot(a, b):
    return jnp.dot(a, b, preferred_element_type=jnp.float32)


def col_max(parts):
    top = jnp.max(parts[0], axis=0, keepdims=True)
    for part in parts[1:]:
        top = jnp.maximum(top, jnp.max(part, axis=0, keepdims=True))
    return top


def weight(scores, top):
    return jnp.exp((scores - top).astype(jnp.bfloat16))


def staggered(steps, scores, weigh, finish):
    ready, weighed = {}, {}
    count = len(steps)
    for at in range(count + 2):
        if at < count:
            ready[at] = scores(steps[at])
        if 0 <= at - 1 < count:
            weighed[at - 1] = weigh(steps[at - 1], ready.pop(at - 1))
        if 0 <= at - 2 < count:
            finish(steps[at - 2], *weighed.pop(at - 2))


def shared(acc):
    return acc[:HEAD_SIZE] * (1.0 / acc[HEAD_SIZE : HEAD_SIZE + 1])


def body(
    n, levels,
    q_hbm, kv_hbm, res_hbm, extent_hbm, mask_hbm, wo1_hbm, wq2_hbm, wkv2_hbm, wo2_hbm,
    out_ref,
    q, kv, res, wo1, wq2, wkv2, wo2, qx, halo, own2, came, kb, vt, tops, accs, att, hid, norm,
    extent, mask, local_sem, send_sem, recv_sem, enter_sem,
):
    rows = q.shape[0]
    tiles = rows // WIDE
    pairs = q.shape[1] // WIDE
    group_heads = pairs
    heads = list(range(2 * pairs))
    bf16, f32 = jnp.bfloat16, jnp.float32
    scaled = bf16(HEAD_SIZE ** (-0.5))
    me = lax.axis_index("seq")
    loads = {
        name: pltpu.make_async_copy(src, dst, local_sem.at[i])
        for i, (name, src, dst) in enumerate(
            (
                ("kv", kv_hbm, kv),
                ("q", q_hbm, q),
                ("extent", extent_hbm, extent),
                ("mask", mask_hbm, mask),
                ("wo1", wo1_hbm, wo1),
                ("res", res_hbm, res),
                ("wkv2", wkv2_hbm, wkv2),
                ("wq2", wq2_hbm, wq2),
                ("wo2", wo2_hbm, wo2),
            )
        )
    }
    barrier = pltpu.get_barrier_semaphore()
    has_left, has_right = me > 0, me < n - 1

    def partner(level):
        bit = lax.rem(lax.div(me, 1 << level), 2)
        return me + (1 << level) * (1 - 2 * bit)

    def tell(sem, reach):
        @pl.when(me >= reach)
        def _():
            pl.semaphore_signal(sem, inc=1, device_id={"seq": me - reach}, device_id_type=MESH)

        @pl.when(me < n - reach)
        def _():
            pl.semaphore_signal(sem, inc=1, device_id={"seq": me + reach}, device_id_type=MESH)

    def told(sem, reach):
        pl.semaphore_wait(sem, (me >= reach).astype(jnp.int32) + (me < n - reach).astype(jnp.int32))

    tell(barrier, 1)
    for load in loads.values():
        load.start()

    def to_right(near):
        slot = 1 if near else 0
        return pltpu.make_async_remote_copy(
            kv_hbm.at[pl.ds(slot * WIDE, WIDE)], halo.at[slot], send_sem.at[slot], recv_sem.at[slot],
            device_id={"seq": me + 1}, device_id_type=MESH,
        )

    def to_left(near):
        slot = 2 if near else 3
        return pltpu.make_async_remote_copy(
            kv_hbm.at[pl.ds((slot - 2) * WIDE, WIDE)], halo.at[slot], send_sem.at[slot], recv_sem.at[slot],
            device_id={"seq": me - 1}, device_id_type=MESH,
        )

    told(barrier, 1)
    for near in (True, False):

        @pl.when(has_right)
        def _():
            to_right(near).start()

        @pl.when(has_left)
        def _():
            to_left(near).start()

    stages = max(levels - 1, 0)

    def go_on(stage):
        if stage < stages:
            told(enter_sem.at[stage], 1 << stage)
            if stage + 1 < stages:
                tell(enter_sem.at[stage + 1], 1 << (stage + 1))

    if stages:
        tell(enter_sem.at[0], 1)

    for piece in range(vt.shape[0]):
        for group in range(2):
            vt[piece, group, HEAD_SIZE:] = jnp.ones((TOTALS, WIDE), bf16)

    @pl.when(jnp.logical_not(has_left))
    def _():
        halo[0:2] = jnp.zeros((2, *halo.shape[1:]), bf16)

    @pl.when(jnp.logical_not(has_right))
    def _():
        halo[2:4] = jnp.zeros((2, *halo.shape[1:]), bf16)

    def values_in(piece, turned):
        for group in range(2):
            vt[piece, group, :HEAD_SIZE] = turned[group * HEAD_SIZE : (group + 1) * HEAD_SIZE]

    def spread_queries(block):
        low = lax.broadcasted_iota(jnp.int32, (rows, WIDE), 1) < HEAD_SIZE
        none = jnp.zeros((rows, WIDE), bf16)
        for h in heads:
            pair = block[:, h // 2 * WIDE : (h // 2 + 1) * WIDE]
            group = h // group_heads
            if h % 2 != group:
                pair = jnp.concatenate([pair[:, HEAD_SIZE:], pair[:, :HEAD_SIZE]], axis=1)
            qx[h] = jnp.where(low, pair, none) if group == 0 else jnp.where(low, none, pair)

    loads["kv"].wait()
    for t in range(tiles):
        values_in(t, kv[t * WIDE : (t + 1) * WIDE, WIDE:].T)
    loads["q"].wait()
    loads["extent"].wait()
    loads["mask"].wait()
    spread_queries(q[...] * scaled)

    def both(pieces, ref, group):
        return jnp.concatenate([ref[p, group] for p in pieces], axis=1)

    key = lax.broadcasted_iota(jnp.int32, (rows, rows), 0)
    query = lax.broadcasted_iota(jnp.int32, (rows, rows), 1)
    apart = jnp.abs(key - query)

    def own_scores(h):
        return [dot_nt(kv[t * WIDE : (t + 1) * WIDE, :WIDE], qx[h]) for t in range(tiles)]

    def own_weigh(h, parts):
        parts = [
            jnp.where(apart[t * WIDE : (t + 1) * WIDE] <= extent[h], part, HIDE)
            for t, part in enumerate(parts)
        ]
        top = col_max(parts)
        for t in range(tiles):
            tops[t, h] = jnp.broadcast_to(top[:, t * WIDE : (t + 1) * WIDE], tops.shape[2:])
        return (jnp.concatenate([weight(part, top) for part in parts], axis=0),)

    def own_finish(h, shares):
        acc = dot(both(range(tiles), vt, h // group_heads), shares)
        for t in range(tiles):
            accs[t, h] = acc[:, t * WIDE : (t + 1) * WIDE]

    half = len(heads) // 2
    staggered(heads[:half], own_scores, own_weigh, own_finish)
    go_on(0)
    staggered(heads[half:], own_scores, own_weigh, own_finish)
    go_on(1)

    @pl.when(has_left)
    def _():
        to_right(True).wait_recv()

    @pl.when(has_right)
    def _():
        to_left(True).wait_recv()

    for piece in (1, 2):
        values_in(tiles + piece, halo[piece, :, WIDE:].T)

    parity = lax.rem(me, 2)
    order = (1 - parity, parity)
    far = 4 * n * rows
    left_off = jnp.where(has_left, 0, far)
    right_off = jnp.where(has_right, 0, far)
    delta = (
        lax.broadcasted_iota(jnp.int32, (WIDE, WIDE), 1)
        - lax.broadcasted_iota(jnp.int32, (WIDE, WIDE), 0)
    )
    swaps = [
        [
            pltpu.make_async_remote_copy(
                own2.at[t], came.at[level, t],
                send_sem.at[4 + level * tiles + t], recv_sem.at[4 + level * tiles + t],
                device_id={"seq": partner(level)}, device_id_type=MESH,
            )
            for t in order
        ]
        for level in range(levels)
    ]
    halves = []

    def put(h, share, where_to):
        halves.append(share)
        if h % 2:
            pair = jnp.concatenate(halves, axis=0).astype(bf16)
            att[where_to, h // 2 * WIDE : (h // 2 + 1) * WIDE] = pair.T
            halves.clear()

    for name in ("wo1", "res", "wkv2"):
        loads[name].wait()
    for step, t in enumerate(order):
        here = pl.ds(pl.multiple_of(t * WIDE, WIDE), WIDE)
        at_left = t == 0

        @pl.when(jnp.logical_and(at_left, has_left))
        def _():
            to_right(False).wait_recv()

        @pl.when(jnp.logical_and(jnp.logical_not(at_left), has_right))
        def _():
            to_left(False).wait_recv()

        far_piece = 3 * t
        values_in(tiles + far_piece, halo[far_piece, :, WIDE:].T)
        sign = 1 - 2 * t
        off_mid = jnp.where(at_left, left_off, right_off)
        middle = delta * sign

        def side_scores(h):
            return [dot_nt(halo[t + i, :, :WIDE], qx[h, here]) for i in range(3)]

        def side_weigh(h, parts):
            reach = extent[h]
            a = jnp.where(delta <= reach - rows - left_off, parts[0], HIDE)
            b = jnp.where(middle <= reach - WIDE - off_mid, parts[1], HIDE)
            c = jnp.where(delta >= rows + right_off - reach, parts[2], HIDE)
            before = tops[t, h, 0:1]
            top = jnp.maximum(before, col_max([a, b, c]))
            return jnp.exp(before - top), jnp.concatenate([weight(x, top) for x in (a, b, c)], axis=0)

        def side_finish(h, fade, shares):
            lhs = both([tiles + t + i for i in range(3)], vt, h // group_heads)
            put(h, shared(accs[t, h] * fade + dot(lhs, shares)), here)

        staggered(heads, side_scores, side_weigh, side_finish)

        hidden = (dot(att[here], wo1[...]) + res[here].astype(f32)).astype(bf16)
        hid[here] = hidden
        values = hidden.astype(f32)
        scale = lax.rsqrt(jnp.mean(values * values, axis=-1, keepdims=True) + 1e-05)
        normed = (values * scale).astype(bf16)
        norm[here] = normed
        keyvals = dot(normed, wkv2[...]).astype(bf16)
        own2[t, :WIDE] = keyvals[:, :WIDE]
        own2[t, WIDE:] = keyvals[:, WIDE:].T
        if step == 0:
            for stage in range(2, stages):
                go_on(stage)
        for swap in reversed(swaps):
            swap[step].start()

    loads["wq2"].wait()
    spread_queries(dot(norm[...], wq2[...]).astype(bf16) * scaled)

    first = [(0, t) for t in range(tiles)]
    chunks = [first]
    if levels > 0:
        chunks = [first + [(1, t) for t in range(tiles)]]
    split = max(1, levels - 2)
    for level in range(1, split):
        chunks.append([(level + 1, t) for t in range(tiles)])
    if levels > split:
        for t in order:
            chunks.append([(level + 1, t) for level in reversed(range(split, levels))])
    last = len(chunks) - 1

    for number, chunk in enumerate(chunks):
        for slot, t in chunk:
            if slot == 0:
                values_in(t, own2[t, WIDE:])
                continue
            level = slot - 1
            pltpu.make_async_remote_copy(
                own2.at[t], came.at[level, t],
                send_sem.at[4 + level * tiles + t], recv_sem.at[4 + level * tiles + t],
                device_id={"seq": partner(level)}, device_id_type=MESH,
            ).wait_recv()
            seen = mask[0, level] == 1
            piece = slot * tiles + t
            kb[level * tiles + t] = jnp.where(seen, came[level, t, :WIDE], own2[t, :WIDE])
            turned = came[level, t, WIDE:]
            values_in(piece, jnp.where(seen, turned, jnp.zeros_like(turned)))
            for group in range(2):
                vt[piece, group, HEAD_SIZE:] = jnp.where(
                    seen, jnp.ones((TOTALS, WIDE), bf16), jnp.zeros((TOTALS, WIDE), bf16)
                )

        def keys_of(slot, t):
            return own2[t, :WIDE] if slot == 0 else kb[(slot - 1) * tiles + t]

        def far_scores(h):
            return [dot_nt(keys_of(slot, t), qx[h]) for slot, t in chunk]

        def far_weigh(h, parts):
            top = col_max(parts)
            fade = None
            if number > 0:
                before = jnp.concatenate([tops[t, h, 0:1] for t in range(tiles)], axis=1)
                top = jnp.maximum(before, top)
                fade = jnp.exp(before - top)
            if number < last:
                for t in range(tiles):
                    tops[t, h] = jnp.broadcast_to(top[:, t * WIDE : (t + 1) * WIDE], tops.shape[2:])
            return fade, [weight(part, top) for part in parts]

        def far_finish(h, fade, parts):
            acc = None
            if fade is not None:
                acc = jnp.concatenate([accs[t, h] for t in range(tiles)], axis=1) * fade
            for i in range(0, len(chunk), 2):
                lhs = both([slot * tiles + t for slot, t in chunk[i : i + 2]], vt, h // group_heads)
                term = dot(lhs, jnp.concatenate(parts[i : i + 2], axis=0))
                acc = term if acc is None else acc + term
            if number < last:
                for t in range(tiles):
                    accs[t, h] = acc[:, t * WIDE : (t + 1) * WIDE]
            else:
                put(h, shared(acc), slice(0, rows))

        staggered(heads, far_scores, far_weigh, far_finish)

    loads["wo2"].wait()
    out_ref[...] = (dot(att[...], wo2[...]) + hid[...].astype(f32)).astype(bf16)
    for level in swaps:
        for swap in level:
            swap.wait_send()
    for near in (True, False):

        @pl.when(has_right)
        def _():
            to_right(near).wait_send()

        @pl.when(has_left)
        def _():
            to_left(near).wait_send()


def shards(
    n, residual, layer_queries, layer_keyvals, head_window_extent, block_mask,
    first_out, second_query, second_keyval, second_out,
):
    levels = n.bit_length() - 1
    rows, width = residual.shape
    query_width = layer_queries.shape[1]
    kv_width = layer_keyvals.shape[1]
    tiles = rows // WIDE
    pieces = max(tiles + 4, (levels + 1) * tiles)
    bf16, f32 = jnp.bfloat16, jnp.float32
    stays = pl.BlockSpec(memory_space=pltpu.HBM)
    return pl.pallas_call(
        functools.partial(body, n, levels),
        name="two_layers",
        out_shape=pltpu.VMEM((rows, width), bf16),
        in_specs=[stays] * 9,
        out_specs=pl.BlockSpec(memory_space=pltpu.VMEM),
        scratch_shapes=[
            pltpu.VMEM((rows, query_width), bf16),
            pltpu.VMEM((rows, kv_width), bf16),
            pltpu.VMEM((rows, width), bf16),
            pltpu.VMEM(first_out.shape, bf16),
            pltpu.VMEM(second_query.shape, bf16),
            pltpu.VMEM(second_keyval.shape, bf16),
            pltpu.VMEM(second_out.shape, bf16),
            pltpu.VMEM((QUERY_HEADS, rows, WIDE), bf16),
            pltpu.VMEM((4, WIDE, kv_width), bf16),
            pltpu.VMEM((tiles, 2 * WIDE, WIDE), bf16),
            pltpu.VMEM((max(levels, 1), tiles, 2 * WIDE, WIDE), bf16),
            pltpu.VMEM((max(levels, 1) * tiles, WIDE, WIDE), bf16),
            pltpu.VMEM((pieces, 2, HEAD_SIZE + TOTALS, WIDE), bf16),
            pltpu.VMEM((tiles, QUERY_HEADS, 8, WIDE), f32),
            pltpu.VMEM((tiles, QUERY_HEADS, HEAD_SIZE + TOTALS, WIDE), f32),
            pltpu.VMEM((rows, query_width), bf16),
            pltpu.VMEM((rows, width), bf16),
            pltpu.VMEM((rows, width), bf16),
            pltpu.SMEM(head_window_extent.shape, jnp.int32),
            pltpu.SMEM(block_mask.shape, jnp.int32),
            pltpu.SemaphoreType.DMA((9,)),
            pltpu.SemaphoreType.DMA((4 + levels * tiles,)),
            pltpu.SemaphoreType.DMA((4 + levels * tiles,)),
            pltpu.SemaphoreType.REGULAR((max(levels - 1, 1),)),
        ],
        compiler_params=pltpu.CompilerParams(
            collective_id=0, has_side_effects=True
        ),
    )(
        layer_queries, layer_keyvals, residual, head_window_extent, block_mask,
        first_out, second_query, second_keyval, second_out,
    )


def solution(mesh):
    placed = (
        P(("groups", "seq"), None),
        P(("groups", "seq"), None),
        P(("groups", "seq"), None),
        P(),
        P("seq", None),
        P(),
        P(),
        P(),
        P(),
    )
    return jax.shard_map(
        functools.partial(shards, mesh.shape["seq"]),
        mesh=mesh, in_specs=placed, out_specs=P(("groups", "seq"), None), check_vma=False,
    )
```

time: 21.3 us -> 18.8 us (0.88)
  Pallas kernels: 20.4 us -> 17.9 us
    pallas_call x1, Pallas kernels: 20.4 us -> 17.9 us  [shards(): pl.pallas_call(functools.partial(body, n, levels), name='two_layers', out...]
where the time goes in v2:
time: 18.8 us; the launch traced here: 18.7 us
  Pallas kernels  17.9 us (95%)
  local copies, waits for them, and re-layouts  0.8 us (4%)
    pallas_call x1, Pallas kernels, shards(): pl.pallas_call(functools.partial(body, n, levels), name='two_layers', out...  17.9 us
    unnamed x1, local copies, waits for them, and re-layouts  0.8 us

profile of v2, /device:TPU:0, one launch (start us, length us, event | category | flops | bytes accessed | tf_op | source)
XLA Modules:
  0.0 18.7 jit_solution(11572205721248000574)
XLA Ops:
  0.0 17.9 %two_layers.1 = bf16[256,1024]{1,0:T(8,128)(2,1)S(1)} custom-call(bf16[256,512]{1,0:T(8,128)(2,1)} %q_hbm.1, bf16[256,256]{1,0:T(8,128)(2,1)} %kv_hbm.1, bf16[256,1024]{1,0:T(8,128)(2,1)} %res_hbm.1, s32[8]{0:T(128)} %extent_hbm.1, s32[1,4]{1,0:T(1,128)} %mask_hbm.1, bf16[512,1024]{1,0:T(8,128)(2,1)} %wo1_hbm.1, bf16[1024,512]{1,0:T(8,128)(2,1)} %wq2_hbm.1, ...), custom_call_target="tpu_custom_call" | custom-call | tf_op jit(solution)/shard_map/two_layers/pallas_call | solution.py:400
  17.9 0.8 %copy.11 = bf16[256,1024]{1,0:T(8,128)(2,1)} copy(bf16[256,1024]{1,0:T(8,128)(2,1)S(1)} %two_layers.1) | data formatting | bytes 1048576

commit v3 on v2

--- a/solution.py
+++ b/solution.py
@@ -13,11 +13,6 @@
 MESH = pl.DeviceIdType.MESH
 HIDE = -1e30
 TOTALS = 16
-NT = (((1,), (1,)), ((), ()))
-
-
-def dot_nt(a, b):
-    return lax.dot_general(a, b, NT, preferred_element_type=jnp.float32)
 
 
 def dot(a, b):
@@ -158,14 +153,20 @@
             vt[piece, group, :HEAD_SIZE] = turned[group * HEAD_SIZE : (group + 1) * HEAD_SIZE]
 
     def spread_queries(block):
-        low = lax.broadcasted_iota(jnp.int32, (rows, WIDE), 1) < HEAD_SIZE
-        none = jnp.zeros((rows, WIDE), bf16)
-        for h in heads:
-            pair = block[:, h // 2 * WIDE : (h // 2 + 1) * WIDE]
-            group = h // group_heads
-            if h % 2 != group:
-                pair = jnp.concatenate([pair[:, HEAD_SIZE:], pair[:, :HEAD_SIZE]], axis=1)
-            qx[h] = jnp.where(low, pair, none) if group == 0 else jnp.where(low, none, pair)
+        for pair in range(pairs):
+            for t in range(tiles):
+                turned = block[t * WIDE : (t + 1) * WIDE, pair * WIDE : (pair + 1) * WIDE].T
+                for h in (2 * pair, 2 * pair + 1):
+                    group = h // group_heads
+                    start = group * HEAD_SIZE
+                    qx[t, h, start : start + HEAD_SIZE] = turned[h % 2 * HEAD_SIZE : (h % 2 + 1) * HEAD_SIZE]
+
+    for h in heads:
+        start = (1 - h // group_heads) * HEAD_SIZE
+        qx[:, h, start : start + HEAD_SIZE] = jnp.zeros((tiles, HEAD_SIZE, WIDE), bf16)
+
+    def queries_of(h):
+        return jnp.concatenate([qx[t, h] for t in range(tiles)], axis=1)
 
     loads["kv"].wait()
     for t in range(tiles):
@@ -183,17 +184,14 @@
     apart = jnp.abs(key - query)
 
     def own_scores(h):
-        return [dot_nt(kv[t * WIDE : (t + 1) * WIDE, :WIDE], qx[h]) for t in range(tiles)]
+        return (dot(kv[:, :WIDE], queries_of(h)),)
 
     def own_weigh(h, parts):
-        parts = [
-            jnp.where(apart[t * WIDE : (t + 1) * WIDE] <= extent[h], part, HIDE)
-            for t, part in enumerate(parts)
-        ]
-        top = col_max(parts)
+        scores = jnp.where(apart <= extent[h], parts[0], HIDE)
+        top = col_max([scores])
         for t in range(tiles):
             tops[t, h] = jnp.broadcast_to(top[:, t * WIDE : (t + 1) * WIDE], tops.shape[2:])
-        return (jnp.concatenate([weight(part, top) for part in parts], axis=0),)
+        return (weight(scores, top),)
 
     def own_finish(h, shares):
         acc = dot(both(range(tiles), vt, h // group_heads), shares)
@@ -266,23 +264,39 @@
         off_mid = jnp.where(at_left, left_off, right_off)
         middle = delta * sign
 
+        def twice(ref, h):
+            return jnp.concatenate([ref[t, h], ref[t, h + 1]], axis=1)
+
         def side_scores(h):
-            return [dot_nt(halo[t + i, :, :WIDE], qx[h, here]) for i in range(3)]
+            keys = jnp.concatenate([halo[t + i, :, :WIDE] for i in range(3)], axis=0)
+            scores = dot(keys, twice(qx, h))
+            return [scores[i * WIDE : (i + 1) * WIDE] for i in range(3)]
 
         def side_weigh(h, parts):
-            reach = extent[h]
-            a = jnp.where(delta <= reach - rows - left_off, parts[0], HIDE)
-            b = jnp.where(middle <= reach - WIDE - off_mid, parts[1], HIDE)
-            c = jnp.where(delta >= rows + right_off - reach, parts[2], HIDE)
-            before = tops[t, h, 0:1]
-            top = jnp.maximum(before, col_max([a, b, c]))
-            return jnp.exp(before - top), jnp.concatenate([weight(x, top) for x in (a, b, c)], axis=0)
+            kept = []
+            for k in range(2):
+                reach = extent[h + k]
+                a, b, c = (part[:, k * WIDE : (k + 1) * WIDE] for part in parts)
+                kept.append((
+                    jnp.where(delta <= reach - rows - left_off, a, HIDE),
+                    jnp.where(middle <= reach - WIDE - off_mid, b, HIDE),
+                    jnp.where(delta >= rows + right_off - reach, c, HIDE),
+                ))
+            shares, fades = [], []
+            for k in range(2):
+                before = tops[t, h + k, 0:1]
+                top = jnp.maximum(before, col_max(kept[k]))
+                fades.append(jnp.exp(before - top))
+                shares.append(jnp.concatenate([weight(x, top) for x in kept[k]], axis=0))
+            return jnp.concatenate(fades, axis=1), jnp.concatenate(shares, axis=1)
 
         def side_finish(h, fade, shares):
             lhs = both([tiles + t + i for i in range(3)], vt, h // group_heads)
-            put(h, shared(accs[t, h] * fade + dot(lhs, shares)), here)
-
-        staggered(heads, side_scores, side_weigh, side_finish)
+            acc = twice(accs, h) * fade + dot(lhs, shares)
+            for k in range(2):
+                put(h + k, shared(acc[:, k * WIDE : (k + 1) * WIDE]), here)
+
+        staggered(heads[::2], side_scores, side_weigh, side_finish)
 
         hidden = (dot(att[here], wo1[...]) + res[here].astype(f32)).astype(bf16)
         hid[here] = hidden
@@ -306,12 +320,15 @@
     chunks = [first]
     if levels > 0:
         chunks = [first + [(1, t) for t in range(tiles)]]
-    split = max(1, levels - 2)
-    for level in range(1, split):
-        chunks.append([(level + 1, t) for t in range(tiles)])
-    if levels > split:
-        for t in order:
-            chunks.append([(level + 1, t) for level in reversed(range(split, levels))])
+    a, b = order
+    later = [(level + 1, t) for level in range(1, levels - 2) for t in order]
+    if levels > 2:
+        later.append((levels - 1, a))
+    chunks += [later[i : i + 3] for i in range(0, len(later), 3)]
+    if levels > 2:
+        chunks += [[(levels, a), (levels - 1, b)], [(levels, b)]]
+    elif levels == 2:
+        chunks += [[(levels, a)], [(levels, b)]]
     last = len(chunks) - 1
 
     for number, chunk in enumerate(chunks):
@@ -339,7 +356,9 @@
             return own2[t, :WIDE] if slot == 0 else kb[(slot - 1) * tiles + t]
 
         def far_scores(h):
-            return [dot_nt(keys_of(slot, t), qx[h]) for slot, t in chunk]
+            keys = jnp.concatenate([keys_of(slot, t) for slot, t in chunk], axis=0)
+            scores = dot(keys, queries_of(h))
+            return [scores[i * WIDE : (i + 1) * WIDE] for i in range(len(chunk))]
 
         def far_weigh(h, parts):
             top = col_max(parts)
@@ -411,7 +430,7 @@
             pltpu.VMEM(second_query.shape, bf16),
             pltpu.VMEM(second_keyval.shape, bf16),
             pltpu.VMEM(second_out.shape, bf16),
-            pltpu.VMEM((QUERY_HEADS, rows, WIDE), bf16),
+            pltpu.VMEM((tiles, QUERY_HEADS, WIDE, WIDE), bf16),
             pltpu.VMEM((4, WIDE, kv_width), bf16),
             pltpu.VMEM((tiles, 2 * WIDE, WIDE), bf16),
             pltpu.VMEM((max(levels, 1), tiles, 2 * WIDE, WIDE), bf16),

time: 18.8 us -> 18.7 us (level)
  Pallas kernels: 17.9 us -> 17.7 us
where the time goes in v3:
time: 18.7 us; the launch traced here: 18.5 us
  Pallas kernels  17.7 us (95%)
  local copies, waits for them, and re-layouts  0.8 us (4%)
    pallas_call x1, Pallas kernels, shards(): pl.pallas_call(functools.partial(body, n, levels), name='two_layers', out...  17.7 us
    unnamed x1, local copies, waits for them, and re-layouts  0.8 us

profile of v3, /device:TPU:0, one launch (start us, length us, event | category | flops | bytes accessed | tf_op | source)
XLA Modules:
  0.0 18.5 jit_solution(6735896742962858661)
XLA Ops:
  0.0 17.7 %two_layers.1 = bf16[256,1024]{1,0:T(8,128)(2,1)S(1)} custom-call(bf16[256,512]{1,0:T(8,128)(2,1)} %q_hbm.1, bf16[256,256]{1,0:T(8,128)(2,1)} %kv_hbm.1, bf16[256,1024]{1,0:T(8,128)(2,1)} %res_hbm.1, s32[8]{0:T(128)} %extent_hbm.1, s32[1,4]{1,0:T(1,128)} %mask_hbm.1, bf16[512,1024]{1,0:T(8,128)(2,1)} %wo1_hbm.1, bf16[1024,512]{1,0:T(8,128)(2,1)} %wq2_hbm.1, ...), custom_call_target="tpu_custom_call" | custom-call | tf_op jit(solution)/shard_map/two_layers/pallas_call | solution.py:419
  17.8 0.8 %copy.11 = bf16[256,1024]{1,0:T(8,128)(2,1)} copy(bf16[256,1024]{1,0:T(8,128)(2,1)S(1)} %two_layers.1) | data formatting | bytes 1048576

commit v4 on v3

--- a/solution.py
+++ b/solution.py
@@ -49,8 +49,8 @@
 def body(
     n, levels,
     q_hbm, kv_hbm, res_hbm, extent_hbm, mask_hbm, wo1_hbm, wq2_hbm, wkv2_hbm, wo2_hbm,
-    out_ref,
-    q, kv, res, wo1, wq2, wkv2, wo2, qx, halo, own2, came, kb, vt, tops, accs, att, hid, norm,
+    att, hid, wo2,
+    q, kv, res, wo1, wq2, wkv2, qx, halo, own2, came, kb, vt, tops, accs, norm,
     extent, mask, local_sem, send_sem, recv_sem, enter_sem,
 ):
     rows = q.shape[0]
@@ -115,8 +115,7 @@
         )
 
     told(barrier, 1)
-    for near in (True, False):
-
+    def send_halo(near):
         @pl.when(has_right)
         def _():
             to_right(near).start()
@@ -124,6 +123,8 @@
         @pl.when(has_left)
         def _():
             to_left(near).start()
+
+    send_halo(True)
 
     stages = max(levels - 1, 0)
 
@@ -175,6 +176,7 @@
     loads["extent"].wait()
     loads["mask"].wait()
     spread_queries(q[...] * scaled)
+    send_halo(False)
 
     def both(pieces, ref, group):
         return jnp.concatenate([ref[p, group] for p in pieces], axis=1)
@@ -389,7 +391,6 @@
         staggered(heads, far_scores, far_weigh, far_finish)
 
     loads["wo2"].wait()
-    out_ref[...] = (dot(att[...], wo2[...]) + hid[...].astype(f32)).astype(bf16)
     for level in swaps:
         for swap in level:
             swap.wait_send()
@@ -402,6 +403,20 @@
         @pl.when(has_left)
         def _():
             to_left(near).wait_send()
+
+
+def project(att, hid, weight_ref, out_hbm, out, sem):
+    width = out.shape[1]
+    step = min(width, 4 * WIDE)
+    copies = []
+    for start in range(0, width, step):
+        here = pl.ds(start, step)
+        total = dot(att[...], weight_ref[:, here]) + hid[:, here].astype(jnp.float32)
+        out[:, here] = total.astype(out.dtype)
+        copies.append(pltpu.make_async_copy(out.at[:, here], out_hbm.at[:, here], sem.at[len(copies)]))
+        copies[-1].start()
+    for copy in copies:
+        copy.wait()
 
 
 def shards(
@@ -416,12 +431,17 @@
     pieces = max(tiles + 4, (levels + 1) * tiles)
     bf16, f32 = jnp.bfloat16, jnp.float32
     stays = pl.BlockSpec(memory_space=pltpu.HBM)
-    return pl.pallas_call(
+    held = pl.BlockSpec(memory_space=pltpu.VMEM)
+    att, hidden, weights = pl.pallas_call(
         functools.partial(body, n, levels),
         name="two_layers",
-        out_shape=pltpu.VMEM((rows, width), bf16),
+        out_shape=(
+            pltpu.VMEM((rows, query_width), bf16),
+            pltpu.VMEM((rows, width), bf16),
+            pltpu.VMEM(second_out.shape, bf16),
+        ),
         in_specs=[stays] * 9,
-        out_specs=pl.BlockSpec(memory_space=pltpu.VMEM),
+        out_specs=(held, held, held),
         scratch_shapes=[
             pltpu.VMEM((rows, query_width), bf16),
             pltpu.VMEM((rows, kv_width), bf16),
@@ -429,7 +449,6 @@
             pltpu.VMEM(first_out.shape, bf16),
             pltpu.VMEM(second_query.shape, bf16),
             pltpu.VMEM(second_keyval.shape, bf16),
-            pltpu.VMEM(second_out.shape, bf16),
             pltpu.VMEM((tiles, QUERY_HEADS, WIDE, WIDE), bf16),
             pltpu.VMEM((4, WIDE, kv_width), bf16),
             pltpu.VMEM((tiles, 2 * WIDE, WIDE), bf16),
@@ -438,8 +457,6 @@
             pltpu.VMEM((pieces, 2, HEAD_SIZE + TOTALS, WIDE), bf16),
             pltpu.VMEM((tiles, QUERY_HEADS, 8, WIDE), f32),
             pltpu.VMEM((tiles, QUERY_HEADS, HEAD_SIZE + TOTALS, WIDE), f32),
-            pltpu.VMEM((rows, query_width), bf16),
-            pltpu.VMEM((rows, width), bf16),
             pltpu.VMEM((rows, width), bf16),
             pltpu.SMEM(head_window_extent.shape, jnp.int32),
             pltpu.SMEM(block_mask.shape, jnp.int32),
@@ -455,6 +472,18 @@
         layer_queries, layer_keyvals, residual, head_window_extent, block_mask,
         first_out, second_query, second_keyval, second_out,
     )
+    return pl.pallas_call(
+        project,
+        name="project",
+        out_shape=jax.ShapeDtypeStruct((rows, width), bf16),
+        in_specs=[held] * 3,
+        out_specs=pl.BlockSpec(memory_space=pl.ANY),
+        scratch_shapes=[
+            pltpu.VMEM((rows, width), bf16),
+            pltpu.SemaphoreType.DMA((max(1, width // (4 * WIDE)),)),
+        ],
+        compiler_params=pltpu.CompilerParams(vmem_limit_bytes=16 * 2**20),
+    )(*(pltpu.with_memory_space_constraint(x, pltpu.VMEM) for x in (att, hidden, weights)))
 
 
 def solution(mesh):

time: 18.7 us -> 18.5 us (0.989)
  local copies, waits for them, and re-layouts: 0.8 us -> 0 us
  Pallas kernels: 17.7 us -> 18.3 us
    pallas_call x0 -> x1, Pallas kernels: none -> 1.16 us  [shards(): pl.pallas_call(project, name='project', out_shape=jax.ShapeDtypeStruct((r...]
    unnamed x1 -> x0, local copies, waits for them, and re-layouts: 0.8 us -> none
    pallas_call x1, Pallas kernels: 17.7 us -> 17.2 us  [shards(): pl.pallas_call(functools.partial(body, n, levels), name='two_layers', out...]
where the time goes in v4:
time: 18.5 us; the launch traced here: 18.3 us
  Pallas kernels  18.3 us (99%)
    pallas_call x1, Pallas kernels, shards(): pl.pallas_call(functools.partial(body, n, levels), name='two_layers', out...  17.2 us
    pallas_call x1, Pallas kernels, shards(): pl.pallas_call(project, name='project', out_shape=jax.ShapeDtypeStruct((r...  1.16 us

profile of v4, /device:TPU:0, one launch (start us, length us, event | category | flops | bytes accessed | tf_op | source)
XLA Modules:
  0.0 18.3 jit_solution(10334423999666521768)
XLA Ops:
  0.0 17.2 %two_layers.1 = (bf16[256,512]{1,0:T(8,128)(2,1)S(1)}, bf16[256,1024]{1,0:T(8,128)(2,1)S(1)}, bf16[512,1024]{1,0:T(8,128)(2,1)S(1)}) custom-call(bf16[256,512]{1,0:T(8,128)(2,1)} %q_hbm.1, bf16[256,256]{1,0:T(8,128)(2,1)} %kv_hbm.1, bf16[256,1024]{1,0:T(8,128)(2,1)} %res_hbm.1, s32[8]{0:T(128)} %extent_hbm.1, s32[1,4]{1,0:T(1,128)} %mask_hbm.1, ...), custom_call_target="tpu_custom_call" | custom-call | tf_op jit(solution)/shard_map/two_layers/pallas_call | solution.py:435
  17.2 1.2 %project.1 = bf16[256,1024]{1,0:T(8,128)(2,1)} custom-call(bf16[256,512]{1,0:T(8,128)(2,1)S(1)} %get-tuple-element.8.att, bf16[256,1024]{1,0:T(8,128)(2,1)S(1)} %get-tuple-element.9.hid, bf16[512,1024]{1,0:T(8,128)(2,1)S(1)} %get-tuple-element.10.weight_ref), custom_call_target="tpu_custom_call" | custom-call | tf_op jit(solution)/shard_map/project/pallas_call | solution.py:475

commit v5 on v4

--- a/solution.py
+++ b/solution.py
@@ -103,14 +103,14 @@
     def to_right(near):
         slot = 1 if near else 0
         return pltpu.make_async_remote_copy(
-            kv_hbm.at[pl.ds(slot * WIDE, WIDE)], halo.at[slot], send_sem.at[slot], recv_sem.at[slot],
+            kv_hbm.at[pl.ds(slot * WIDE, WIDE)], halo.at[slot], send_sem.at[0], recv_sem.at[slot],
             device_id={"seq": me + 1}, device_id_type=MESH,
         )
 
     def to_left(near):
         slot = 2 if near else 3
         return pltpu.make_async_remote_copy(
-            kv_hbm.at[pl.ds((slot - 2) * WIDE, WIDE)], halo.at[slot], send_sem.at[slot], recv_sem.at[slot],
+            kv_hbm.at[pl.ds((slot - 2) * WIDE, WIDE)], halo.at[slot], send_sem.at[1], recv_sem.at[slot],
             device_id={"seq": me - 1}, device_id_type=MESH,
         )
 
@@ -230,7 +230,7 @@
         [
             pltpu.make_async_remote_copy(
                 own2.at[t], came.at[level, t],
-                send_sem.at[4 + level * tiles + t], recv_sem.at[4 + level * tiles + t],
+                send_sem.at[2], recv_sem.at[4 + level * tiles + t],
                 device_id={"seq": partner(level)}, device_id_type=MESH,
             )
             for t in order
@@ -341,7 +341,7 @@
             level = slot - 1
             pltpu.make_async_remote_copy(
                 own2.at[t], came.at[level, t],
-                send_sem.at[4 + level * tiles + t], recv_sem.at[4 + level * tiles + t],
+                send_sem.at[2], recv_sem.at[4 + level * tiles + t],
                 device_id={"seq": partner(level)}, device_id_type=MESH,
             ).wait_recv()
             seen = mask[0, level] == 1
@@ -391,18 +391,22 @@
         staggered(heads, far_scores, far_weigh, far_finish)
 
     loads["wo2"].wait()
-    for level in swaps:
-        for swap in level:
-            swap.wait_send()
-    for near in (True, False):
-
-        @pl.when(has_right)
-        def _():
-            to_right(near).wait_send()
-
-        @pl.when(has_left)
-        def _():
-            to_left(near).wait_send()
+    def sent(sem, whole):
+        pltpu.make_async_remote_copy(
+            whole, whole, send_sem.at[sem], recv_sem.at[0],
+            device_id={"seq": partner(0)}, device_id_type=MESH,
+        ).wait_send()
+
+    if levels:
+        sent(2, came)
+
+    @pl.when(has_right)
+    def _():
+        sent(0, halo.at[pl.ds(0, 2)])
+
+    @pl.when(has_left)
+    def _():
+        sent(1, halo.at[pl.ds(0, 2)])
 
 
 def project(att, hid, weight_ref, out_hbm, out, sem):
@@ -461,7 +465,7 @@
             pltpu.SMEM(head_window_extent.shape, jnp.int32),
             pltpu.SMEM(block_mask.shape, jnp.int32),
             pltpu.SemaphoreType.DMA((9,)),
-            pltpu.SemaphoreType.DMA((4 + levels * tiles,)),
+            pltpu.SemaphoreType.DMA((3,)),
             pltpu.SemaphoreType.DMA((4 + levels * tiles,)),
             pltpu.SemaphoreType.REGULAR((max(levels - 1, 1),)),
         ],

time: 18.5 us -> 18.4 us (level)
  no operation moved by 1% of the time
where the time goes in v5:
time: 18.4 us; the launch traced here: 18.2 us
  Pallas kernels  18.2 us (99%)
    pallas_call x1, Pallas kernels, shards(): pl.pallas_call(functools.partial(body, n, levels), name='two_layers', out...  17.1 us
    pallas_call x1, Pallas kernels, shards(): pl.pallas_call(project, name='project', out_shape=jax.ShapeDtypeStruct((r...  1.16 us

profile of v5, /device:TPU:0, one launch (start us, length us, event | category | flops | bytes accessed | tf_op | source)
XLA Modules:
  0.0 18.2 jit_solution(3275912759499792966)
XLA Ops:
  0.0 17.1 %two_layers.1 = (bf16[256,512]{1,0:T(8,128)(2,1)S(1)}, bf16[256,1024]{1,0:T(8,128)(2,1)S(1)}, bf16[512,1024]{1,0:T(8,128)(2,1)S(1)}) custom-call(bf16[256,512]{1,0:T(8,128)(2,1)} %q_hbm.1, bf16[256,256]{1,0:T(8,128)(2,1)} %kv_hbm.1, bf16[256,1024]{1,0:T(8,128)(2,1)} %res_hbm.1, s32[8]{0:T(128)} %extent_hbm.1, s32[1,4]{1,0:T(1,128)} %mask_hbm.1, ...), custom_call_target="tpu_custom_call" | custom-call | tf_op jit(solution)/shard_map/two_layers/pallas_call | solution.py:439
  17.1 1.2 %project.1 = bf16[256,1024]{1,0:T(8,128)(2,1)} custom-call(bf16[256,512]{1,0:T(8,128)(2,1)S(1)} %get-tuple-element.8.att, bf16[256,1024]{1,0:T(8,128)(2,1)S(1)} %get-tuple-element.9.hid, bf16[512,1024]{1,0:T(8,128)(2,1)S(1)} %get-tuple-element.10.weight_ref), custom_call_target="tpu_custom_call" | custom-call | tf_op jit(solution)/shard_map/project/pallas_call | solution.py:479

commit v6 on v5

--- a/solution.py
+++ b/solution.py
@@ -226,11 +226,16 @@
         lax.broadcasted_iota(jnp.int32, (WIDE, WIDE), 1)
         - lax.broadcasted_iota(jnp.int32, (WIDE, WIDE), 0)
     )
+    single = max(levels - 2, 1)
+
+    def landing(level, t):
+        return 4 + level if level < single else 4 + single + (level - single) * tiles + t
+
     swaps = [
         [
             pltpu.make_async_remote_copy(
                 own2.at[t], came.at[level, t],
-                send_sem.at[2], recv_sem.at[4 + level * tiles + t],
+                send_sem.at[2], recv_sem.at[landing(level, t)],
                 device_id={"seq": partner(level)}, device_id_type=MESH,
             )
             for t in order
@@ -332,6 +337,7 @@
     elif levels == 2:
         chunks += [[(levels, a)], [(levels, b)]]
     last = len(chunks) - 1
+    landed = set()
 
     for number, chunk in enumerate(chunks):
         for slot, t in chunk:
@@ -339,11 +345,13 @@
                 values_in(t, own2[t, WIDE:])
                 continue
             level = slot - 1
-            pltpu.make_async_remote_copy(
-                own2.at[t], came.at[level, t],
-                send_sem.at[2], recv_sem.at[4 + level * tiles + t],
-                device_id={"seq": partner(level)}, device_id_type=MESH,
-            ).wait_recv()
+            if level >= single or level not in landed:
+                here = came.at[level] if level < single else came.at[level, t]
+                pltpu.make_async_remote_copy(
+                    here, here, send_sem.at[2], recv_sem.at[landing(level, t)],
+                    device_id={"seq": partner(level)}, device_id_type=MESH,
+                ).wait_recv()
+                landed.add(level)
             seen = mask[0, level] == 1
             piece = slot * tiles + t
             kb[level * tiles + t] = jnp.where(seen, came[level, t, :WIDE], own2[t, :WIDE])

time: 18.4 us -> 18.4 us (level)
  no operation moved by 1% of the time
where the time goes in v6:
time: 18.4 us; the launch traced here: 18.2 us
  Pallas kernels  18.2 us (99%)
    pallas_call x1, Pallas kernels, shards(): pl.pallas_call(functools.partial(body, n, levels), name='two_layers', out...  17.1 us
    pallas_call x1, Pallas kernels, shards(): pl.pallas_call(project, name='project', out_shape=jax.ShapeDtypeStruct((r...  1.16 us

profile of v6, /device:TPU:0, one launch (start us, length us, event | category | flops | bytes accessed | tf_op | source)
XLA Modules:
  0.0 18.2 jit_solution(5471499446524017294)
XLA Ops:
  0.0 17.1 %two_layers.1 = (bf16[256,512]{1,0:T(8,128)(2,1)S(1)}, bf16[256,1024]{1,0:T(8,128)(2,1)S(1)}, bf16[512,1024]{1,0:T(8,128)(2,1)S(1)}) custom-call(bf16[256,512]{1,0:T(8,128)(2,1)} %q_hbm.1, bf16[256,256]{1,0:T(8,128)(2,1)} %kv_hbm.1, bf16[256,1024]{1,0:T(8,128)(2,1)} %res_hbm.1, s32[8]{0:T(128)} %extent_hbm.1, s32[1,4]{1,0:T(1,128)} %mask_hbm.1, ...), custom_call_target="tpu_custom_call" | custom-call | tf_op jit(solution)/shard_map/two_layers/pallas_call | solution.py:447
  17.1 1.2 %project.1 = bf16[256,1024]{1,0:T(8,128)(2,1)} custom-call(bf16[256,512]{1,0:T(8,128)(2,1)S(1)} %get-tuple-element.8.att, bf16[256,1024]{1,0:T(8,128)(2,1)S(1)} %get-tuple-element.9.hid, bf16[512,1024]{1,0:T(8,128)(2,1)S(1)} %get-tuple-element.10.weight_ref), custom_call_target="tpu_custom_call" | custom-call | tf_op jit(solution)/shard_map/project/pallas_call | solution.py:487

commit v7 on v5

--- a/solution.py
+++ b/solution.py
@@ -411,10 +411,12 @@
 
 def project(att, hid, weight_ref, out_hbm, out, sem):
     width = out.shape[1]
-    step = min(width, 4 * WIDE)
+    last = min(width, 2 * WIDE)
     copies = []
-    for start in range(0, width, step):
-        here = pl.ds(start, step)
+    for start, size in ((0, width - last), (width - last, last)):
+        if size == 0:
+            continue
+        here = pl.ds(start, size)
         total = dot(att[...], weight_ref[:, here]) + hid[:, here].astype(jnp.float32)
         out[:, here] = total.astype(out.dtype)
         copies.append(pltpu.make_async_copy(out.at[:, here], out_hbm.at[:, here], sem.at[len(copies)]))
@@ -484,7 +486,7 @@
         out_specs=pl.BlockSpec(memory_space=pl.ANY),
         scratch_shapes=[
             pltpu.VMEM((rows, width), bf16),
-            pltpu.SemaphoreType.DMA((max(1, width // (4 * WIDE)),)),
+            pltpu.SemaphoreType.DMA((2,)),
         ],
         compiler_params=pltpu.CompilerParams(vmem_limit_bytes=16 * 2**20),
     )(*(pltpu.with_memory_space_constraint(x, pltpu.VMEM) for x in (att, hidden, weights)))

time: 18.4 us -> 18.5 us (level)
  no operation moved by 1% of the time
where the time goes in v7:
time: 18.5 us; the launch traced here: 18.3 us
  Pallas kernels  18.3 us (99%)
    pallas_call x1, Pallas kernels, shards(): pl.pallas_call(functools.partial(body, n, levels), name='two_layers', out...  17.1 us
    pallas_call x1, Pallas kernels, shards(): pl.pallas_call(project, name='project', out_shape=jax.ShapeDtypeStruct((r...  1.25 us

profile of v7, /device:TPU:0, one launch (start us, length us, event | category | flops | bytes accessed | tf_op | source)
XLA Modules:
  0.0 18.3 jit_solution(10733605797080768145)
XLA Ops:
  0.0 17.1 %two_layers.1 = (bf16[256,512]{1,0:T(8,128)(2,1)S(1)}, bf16[256,1024]{1,0:T(8,128)(2,1)S(1)}, bf16[512,1024]{1,0:T(8,128)(2,1)S(1)}) custom-call(bf16[256,512]{1,0:T(8,128)(2,1)} %q_hbm.1, bf16[256,256]{1,0:T(8,128)(2,1)} %kv_hbm.1, bf16[256,1024]{1,0:T(8,128)(2,1)} %res_hbm.1, s32[8]{0:T(128)} %extent_hbm.1, s32[1,4]{1,0:T(1,128)} %mask_hbm.1, ...), custom_call_target="tpu_custom_call" | custom-call | tf_op jit(solution)/shard_map/two_layers/pallas_call | solution.py:441
  17.1 1.2 %project.1 = bf16[256,1024]{1,0:T(8,128)(2,1)} custom-call(bf16[256,512]{1,0:T(8,128)(2,1)S(1)} %get-tuple-element.8.att, bf16[256,1024]{1,0:T(8,128)(2,1)S(1)} %get-tuple-element.9.hid, bf16[512,1024]{1,0:T(8,128)(2,1)S(1)} %get-tuple-element.10.weight_ref), custom_call_target="tpu_custom_call" | custom-call | tf_op jit(solution)/shard_map/project/pallas_call | solution.py:481
